TPU v7x, 512 devices: a whole 4x8x8 slice. The times are simulated.
512 devices in a mesh: pb: 16 (over y, core), ka: 32 (over x, z).
Axes of the slice: x: 4, y: 8, z: 8, core: 2. Of those that a mesh axis runs over, the one named last changes fastest.
Arguments:
- coupling: bfloat16 [16, 1728, 2, 1600], P('pb', 'ka'), may hold values from -6 to 6
- rot_k: bfloat16 [1728, 2, 1600], P('ka'), may hold values from -0.625 to 0.625
- rot_kq: bfloat16 [16, 1728, 2, 1600], P('pb', 'ka'), may hold values from -0.625 to 0.625
- r_elec: int32 [2048, 3], replicated, may hold values from -6 to 6
- degen: int32 [2048], replicated, may hold values from 1 to 8
- reader: int32 [2048, 1], replicated, may hold values from 0 to 31; in each aligned block of 2048 rows (0 to 2047, 2048 to 4095, ...) at most 128 rows name the same one
- r_phon: int32 [32, 3], replicated, may hold values from -3 to 3
Outputs:
- wannier: float32 [32, 2, 1600, 4096], P(None, None, 'pb', 'ka')
Inputs may be any that keep to these rules, and one draw needn't show every extreme that they name: Each reader is named by at most 128 lattice vectors, and one reader by exactly 128.
All inputs are finite; a program needn't handle non-finite values.
Results may differ from a plain program's by a relative error of at most 0.0056.
Values may be sent and summed in bfloat16 or wider, within the bound.
A program may use at most 128 MiB of HBM per device.

v0:
```python
import math

import jax
import jax.numpy as jnp
from jax import lax
from jax.sharding import PartitionSpec as P

W = 40
KGRID = 12
QGRID = 6


def angle_tables(vectors, count, grid):
    index = jnp.arange(count, dtype=jnp.int32)
    first = index // (grid * grid)
    second = index // grid % grid
    third = index % grid
    inner = (
        vectors[:, 0:1] * first[None, :]
        + vectors[:, 1:2] * second[None, :]
        + vectors[:, 2:3] * third[None, :]
    )
    angle = jnp.mod(inner, grid).astype(jnp.float32) * (2.0 * math.pi / grid)
    return (jnp.cos(angle).astype(jnp.bfloat16), jnp.sin(angle).astype(jnp.bfloat16))


def slot_tables(reader, degen, readers, most):
    reader_row = reader[:, 0]
    member = (reader_row[:, None] == jnp.arange(readers, dtype=jnp.int32)[None, :]).astype(
        jnp.int32
    )
    ranking = jnp.sum((jnp.cumsum(member, axis=0) - 1) * member, axis=1)
    position = reader_row * most + ranking
    source_row = (
        jnp.full((readers * most,), -1, jnp.int32)
        .at[position]
        .set(jnp.arange(reader_row.shape[0], dtype=jnp.int32))
    )
    usable = source_row >= 0
    source_row = jnp.maximum(source_row, 0)
    inverse_deg = jnp.where(usable, 1.0 / degen[source_row].astype(jnp.float32), jnp.float32(0.0))
    return (position, source_row, usable, inverse_deg)


def product(spec, left, right):
    return jnp.einsum(spec, left, right, preferred_element_type=jnp.float32)


def rotate(coupling, rot_k, rot_kq):
    q_local, k_local = (coupling.shape[0], coupling.shape[1])
    g_mat = coupling.reshape(q_local, k_local, 2, W, W)
    u_mat = rot_k.reshape(k_local, 2, W, W)
    v_mat = rot_kq.reshape(q_local, k_local, 2, W, W)
    spec = "qkab,kbn->qkan"
    x_real = product(spec, g_mat[:, :, 0], u_mat[:, 0]) - product(spec, g_mat[:, :, 1], u_mat[:, 1])
    x_imag = product(spec, g_mat[:, :, 0], u_mat[:, 1]) + product(spec, g_mat[:, :, 1], u_mat[:, 0])
    x_real = x_real.astype(jnp.bfloat16)
    x_imag = x_imag.astype(jnp.bfloat16)
    spec_two = "qkam,qkan->qkmn"
    y_real = product(spec_two, v_mat[:, :, 0], x_real) + product(spec_two, v_mat[:, :, 1], x_imag)
    y_imag = product(spec_two, v_mat[:, :, 0], x_imag) - product(spec_two, v_mat[:, :, 1], x_real)
    return jnp.stack([y_real, y_imag], 2).reshape(q_local, k_local, 2, W * W).astype(jnp.bfloat16)


def per_device(coupling, rot_k, rot_kq, r_elec, degen, reader, r_phon):
    ka_count = lax.axis_size("ka")
    pb_count = lax.axis_size("pb")
    q_local, k_local, width_sq = (coupling.shape[0], coupling.shape[1], coupling.shape[3])
    total_k = k_local * ka_count
    total_r = r_elec.shape[0]
    most = 2 * total_r // ka_count
    scale = total_k ** (-0.5)
    rotated = rotate(coupling, rot_k, rot_kq)
    position, source_row, usable, inverse_deg = slot_tables(reader, degen, ka_count, most)
    offset = lax.axis_index("ka") * most
    my_rows = lax.dynamic_slice_in_dim(source_row, offset, most)
    my_usable = lax.dynamic_slice_in_dim(usable, offset, most)
    my_vectors = r_elec[my_rows]
    keep = my_usable.astype(jnp.bfloat16)[:, None]
    span = q_local * width_sq
    piece = lax.all_gather(rotated, "ka", axis=1, tiled=True)
    count = piece.shape[1]
    cosine, sine = angle_tables(my_vectors, count, KGRID)
    left = jnp.concatenate([cosine * keep, sine * keep], axis=1)
    z_real = piece[:, :, 0].transpose(1, 0, 2).reshape(count, span)
    z_imag = piece[:, :, 1].transpose(1, 0, 2).reshape(count, span)
    upper = jnp.concatenate([z_real, z_imag], axis=1)
    lower = jnp.concatenate([z_imag, -z_real], axis=1)
    right = jnp.concatenate([upper, lower], axis=0)
    summed = jnp.dot(left, right, preferred_element_type=jnp.float32)
    real_sum = summed[:, :span]
    imag_sum = summed[:, span:]
    stacked = jnp.stack(
        [real_sum.reshape(most, q_local, width_sq), imag_sum.reshape(most, q_local, width_sq)], 2
    )
    mine = (stacked * scale).astype(jnp.bfloat16)
    gathered_q = lax.all_to_all(mine, "pb", split_axis=3, concat_axis=1, tiled=True)
    total_q = q_local * pb_count
    slim = gathered_q.shape[3]
    phonon_count = r_phon.shape[0]
    q_cos, q_sin = angle_tables(r_phon, total_q, QGRID)
    flat = gathered_q.transpose(1, 0, 2, 3).reshape(total_q, most * 2 * slim)
    c_part = jnp.dot(q_cos, flat, preferred_element_type=jnp.float32).reshape(
        phonon_count, most, 2, slim
    )
    s_part = jnp.dot(q_sin, flat, preferred_element_type=jnp.float32).reshape(
        phonon_count, most, 2, slim
    )
    real_out = c_part[:, :, 0] + s_part[:, :, 1]
    imag_out = c_part[:, :, 1] - s_part[:, :, 0]
    result = jnp.stack([real_out, imag_out], 1).transpose(0, 1, 3, 2)
    my_inverse = lax.dynamic_slice_in_dim(inverse_deg, offset, most)
    return result * (my_inverse * total_q ** (-0.5))[None, None, None, :]


def solution(mesh):
    in_specs = (
        P("pb", "ka", None, None),
        P("ka", None, None),
        P("pb", "ka", None, None),
        P(),
        P(),
        P(),
        P(),
    )
    out_specs = P(None, None, "pb", "ka")
    return jax.shard_map(
        per_device, mesh=mesh, in_specs=in_specs, out_specs=out_specs, check_vma=False
    )
```

profile of v0, /device:TPU:1, one launch (start us, length us, event | category | flops | bytes accessed | tf_op | source)
XLA Modules:
  0.0 320.0 jit_solution(17944751337558424967)
XLA Ops:
  6.5 1.1 copy.55
  7.6 1.0 reshape.274
  8.7 1.7 reshape.311
  10.8 1.5 fusion.29
  12.3 1.3 fusion.19
  14.4 2.0 reshape.278
  16.4 1.8 fusion.18
  19.6 1.0 copy.58
  20.7 1.5 stack.21
  24.6 9.1 %reduce-window.6 = s32[32,16,128]{2,1,0:T(8,128)S(1)} reduce-window(s32[32,16,128]{2,1,0:T(8,128)S(1)} %fusion.36, s32[]{:T(128)} %constant.88.clone.1), window={size=1x1x128 pad=0_0x0_0x127_0}, to_apply=%region_0.0 | reduce-window | flops 8323072 | bytes 524292 | tf_op jit(solution)/shard_map/reduce-window
  34.9 8.2 %scatter_custom_fusion = s32[4096]{0:T(1024)S(1)} fusion(s32[2048]{0:T(1024)S(1)} %bitcast.125, s32[2048]{0:T(1024)S(1)} %iota.45, s32[]{:T(128)} %constant.90.clone.1), kind=kCustom, calls=%fused_computation.94 | custom fusion | bytes 16388 | tf_op jit(solution)/shard_map/scatter | solution.py:37
  44.2 4.3 %fusion.32 = (bf16[128,1728]{1,0:T(8,128)(2,1)S(1)}, bf16[128,1728]{1,0:T(8,128)(2,1)S(1)}) fusion(s32[1728]{0:T(1024)S(1)} %get-tuple-element.21, s32[128]{0:T(128)S(1)} %get-tuple-element.7, s32[1728]{0:T(1024)S(1)} %get-tuple-element.22, s32[128]{0:T(128)S(1)} %get-tuple-element.6, s32[1728]{0:T(1024)S(1)} %add_select_fusion.4, ...), kind=kLoop, calls=%fused_computation.56 | loop fusion | flops 4866048 | bytes 907264 | tf_op jit(solution)/shard_map/mul | solution.py:84
  48.5 100.7 %all-gather.2.cloned.1.call-done = bf16[1,1728,2,1600]{3,2,0,1:T(2,128)(2,1)} async-done(((bf16[1,54,2,1600]{3,2,0,1:T(2,128)(2,1)}), bf16[1,1728,2,1600]{3,2,0,1:T(2,128)(2,1)}) %all-gather.2.cloned.1.call-update) | async-done | bytes 11059216 | tf_op jit(solution)/shard_map/all_gather | solution.py:81
  149.2 23.0 %fusion.69 = (bf16[1,1728,1,1600]{3,2,0,1:T(2,128)(2,1)}, bf16[1,1728,1,1600]{3,2,0,1:T(2,128)(2,1)}) fusion(bf16[1,1728,2,1600]{3,2,0,1:T(2,128)(2,1)} %all-gather.2.cloned.1.call-done), kind=kLoop, calls=%fused_computation.131 | loop fusion | bytes 22118400 | tf_op jit(solution)/shard_map/slice | solution.py:86
  172.2 25.3 %copy.80 = bf16[1,1728,1,1600]{1,3,2,0:T(8,128)(2,1)} copy(bf16[1,1728,1,1600]{3,2,0,1:T(2,128)(2,1)} %get-tuple-element.9) | data formatting | bytes 11059200
  197.5 5.4 %bitcast_negate_fusion = bf16[1728,1600]{0,1:T(8,128)(2,1)} fusion(bf16[1,1728,1,1600]{1,3,2,0:T(8,128)(2,1)} %copy.80), kind=kLoop, calls=%fused_computation.124 | loop fusion | flops 2764800 | bytes 11059200 | tf_op jit(solution)/shard_map/neg | solution.py:88
  202.9 25.2 %copy.81 = bf16[1,1728,1,1600]{1,3,2,0:T(8,128)(2,1)} copy(bf16[1,1728,1,1600]{3,2,0,1:T(2,128)(2,1)} %get-tuple-element.8) | data formatting | bytes 11059200
  228.1 30.9 %fusion = f32[128,3200]{0,1:T(8,128)S(1)} fusion(bf16[1728,1600]{0,1:T(8,128)(2,1)} %bitcast_negate_fusion, bf16[1728,1600]{0,1:T(8,128)(2,1)} %bitcast.115, bf16[1728,1600]{0,1:T(8,128)(2,1)} %bitcast.114, bf16[128,1728]{1,0:T(8,128)(2,1)S(1)} %get-tuple-element.15, bf16[128,1728]{1,0:T(8,128)(2,1)S(1)} %get-tuple-element.14), kind=kOutput, calls=%fused_computation.3 | convolution fusion | flops 2921398272 | bytes 19111936 | tf_op jit(solution)/shard_map/dot_general | solution.py:90
  259.3 7.8 %copy.65 = bf16[128,1,2,1600]{0,2,1,3:T(2,128)(2,1)} copy(bf16[128,1,2,1600]{0,3,2,1:T(8,128)(2,1)S(1)} %fusion.11) | data formatting | bytes 1638400 | tf_op jit(solution)/shard_map/convert_element_type | solution.py:96
  267.0 8.0 %all-to-all-start = ((bf16[128,1,2,1600]{0,2,1,3:T(2,128)(2,1)}), bf16[128,1,2,1600]{0,2,1,3:T(2,128)(2,1)S(1)}, u32[]{:S(2)}, u32[]{:S(2)}) async-start(bf16[128,1,2,1600]{0,2,1,3:T(2,128)(2,1)} %copy.65), calls=%async_computation | async-start | bytes 1638400 | tf_op jit(solution)/shard_map/all_to_all | solution.py:97
  275.0 23.0 %gather_fusion.1 = s32[4096]{0:T(1024)S(1)} fusion(s32[2048]{0:T(1024)S(1)} %copy-done, s32[4096]{0:T(1024)S(1)} %get-tuple-element.16), kind=kCustom, calls=%fused_computation.1 | custom fusion | bytes 49152 | tf_op jit(solution)/shard_map/gather | solution.py:41
  299.4 2.0 reshape.282
  301.4 4.0 %dot_general.47 = bf16[128,2,100,16]{2,1,0,3:T(2,128)(2,1)S(1)} reshape(bf16[25600,16]{0,1:T(8,128)(2,1)S(1)} %bitcast.117) | data formatting | bytes 1638400 | tf_op jit(solution)/shard_map/dot_general | solution.py:103
  308.9 4.2 %copy.70 = f32[32,2,100,128]{3,1,2,0:T(2,128)} copy(f32[32,2,100,128]{3,0,2,1:T(8,128)S(1)} %fusion.8) | data formatting | bytes 6553600 | tf_op jit(solution)/shard_map/mul | solution.py:113
  (60 shorter events, 12.2 us)
Async XLA Ops:
  6.5 268.5 %copy-start = (s32[2048]{0:T(1024)S(1)}, s32[2048]{0:T(1024)}, u32[]{:S(2)}) copy-start(s32[2048]{0:T(1024)} %param.11) | copy-start | bytes 24580
  6.5 2.1 copy-start.3
  6.5 142.7 %all-gather.2.cloned.1.call-start = ((), (), s32[]{:S(2)}) async-start(), calls=%async_computation.1 | async-start | bytes 11860992 | tf_op jit(solution)/shard_map/all_gather | solution.py:81
  12.3 1.3 copy-start.4
  16.4 1.8 copy-start.1
  19.2 3.1 copy-start.2
  22.7 1.9 copy-start.5
  23.4 10.8 %copy-start.6 = (s32[2048,3]{0,1:T(4,128)S(1)}, s32[2048,3]{0,1:T(4,128)}, u32[]{:S(2)}) copy-start(s32[2048,3]{0,1:T(4,128)} %param.10) | copy-start | bytes 73732
  267.0 31.4 %all-to-all-start = ((bf16[128,1,2,1600]{0,2,1,3:T(2,128)(2,1)}), bf16[128,1,2,1600]{0,2,1,3:T(2,128)(2,1)S(1)}, u32[]{:S(2)}, u32[]{:S(2)}) async-start(bf16[128,1,2,1600]{0,2,1,3:T(2,128)(2,1)} %copy.65), calls=%async_computation | async-start | bytes 1638400 | tf_op jit(solution)/shard_map/all_to_all | solution.py:97
  275.0 23.2 %copy-start.7 = (s32[32,3]{0,1:T(4,128)S(1)}, s32[32,3]{0,1:T(4,128)}, u32[]{:S(2)}) copy-start(s32[32,3]{0,1:T(4,128)} %param.13) | copy-start | bytes 1156
Sparse Core Ops, SparseCore 0:
  24.7 124.4 all-gather.1
where the time goes:
time: 322 us; the launch traced here: 320 us
  local copies, waits for them, and re-layouts  137 us (43%)
  waiting for transfers between devices  101 us (31%)
  matrix products  39.3 us (12%)
  other arithmetic  21 us (7%)
  between operations  13.8 us (4%)
  starting transfers between devices  7.98 us (2%)
    all_gather x1, waiting for transfers between devices, per_device(): piece = lax.all_gather(rotated, 'ka', axis=1, tiled=True)  101 us
    unnamed x21, local copies, waits for them, and re-layouts  52.7 us
    dot_general x1, matrix products, per_device(): summed = jnp.dot(left, right, preferred_element_type=jnp.float32)  30.9 us
    gather x1, local copies, waits for them, and re-layouts, slot_tables(): degen[source_row].astype(jnp.float32)  23 us
    slice x1, local copies, waits for them, and re-layouts, per_device(): z_imag = piece[:, :, 1].transpose(1, 0, 2).reshape(count, span)  23 us
    another operation x2, other arithmetic  9.27 us
    scatter x1, local copies, waits for them, and re-layouts, slot_tables(): source_row = jnp.full((readers * most,), -1, jnp.int32).at[position].set(...  8.24 us
    all_to_all x1, starting transfers between devices, per_device(): lax.all_to_all(mine, 'pb', split_axis=3, concat_axis=1, tiled=True)  7.97 us
  transfers between devices with their start and end apart: 2, of which 2 were waited for; matrix products, arithmetic and copies ran while one was open for 15% of the time, Pallas kernels for 0%

commit v1 on v0

v1 whole, which is shorter than its diff:
```python
import math

import jax
import jax.numpy as jnp
import numpy as np
from jax import lax
from jax.experimental import pallas as pl
from jax.experimental.pallas import tpu as pltpu
from jax.sharding import PartitionSpec as P

W = 40
KGRID = 12
QGRID = 6
READERS = 32
MOST = 128
PLANE = KGRID * KGRID
ROWS = 1792
VMEM = pl.BlockSpec(memory_space=pltpu.VMEM)


def plane_table():
    index = np.arange(PLANE)
    inner = np.outer(index // KGRID, index // KGRID) + np.outer(index % KGRID, index % KGRID)
    angle = (inner % KGRID) * (2.0 * math.pi / KGRID)
    cosine, sine = np.cos(angle), np.sin(angle)
    return np.block([[cosine, sine], [-sine, cosine]]).astype(np.float32).astype(jnp.bfloat16)


def product(spec, left, right):
    return jnp.einsum(spec, left, right, preferred_element_type=jnp.float32)


def rotate(coupling, rot_k, rot_kq):
    k_local = coupling.shape[1]
    g_mat = coupling.reshape(k_local, 2, W, W)
    u_mat = rot_k.reshape(k_local, 2, W, W)
    v_mat = rot_kq.reshape(k_local, 2, W, W)
    spec = "kab,kbn->kan"
    x_real = product(spec, g_mat[:, 0], u_mat[:, 0]) - product(spec, g_mat[:, 1], u_mat[:, 1])
    x_imag = product(spec, g_mat[:, 0], u_mat[:, 1]) + product(spec, g_mat[:, 1], u_mat[:, 0])
    x_real = x_real.astype(jnp.bfloat16)
    x_imag = x_imag.astype(jnp.bfloat16)
    spec_two = "kam,kan->kmn"
    y_real = product(spec_two, v_mat[:, 0], x_real) + product(spec_two, v_mat[:, 1], x_imag)
    y_imag = product(spec_two, v_mat[:, 0], x_imag) - product(spec_two, v_mat[:, 1], x_real)
    return jnp.stack([y_real, y_imag], 1).reshape(k_local, 2, W * W).astype(jnp.bfloat16)


def table_kernel(reader_ref, vector_ref, degen_ref, phonon_ref, residue_ref, inverse_ref, kron_ref):
    total_r = reader_ref.shape[1]
    f32, bf16 = jnp.float32, jnp.bfloat16
    reader_id = lax.broadcasted_iota(jnp.int32, (READERS, 128), 0)
    slot_id = lax.broadcasted_iota(jnp.int32, (MOST, 128), 0)
    before = (
        lax.broadcasted_iota(jnp.int32, (128, 128), 0)
        < lax.broadcasted_iota(jnp.int32, (128, 128), 1)
    ).astype(f32).astype(bf16)
    offset = jnp.zeros((READERS, 1), f32)
    table = jnp.zeros((3 * READERS, MOST), f32)
    for block in range(total_r // 128):
        lanes = slice(block * 128, (block + 1) * 128)
        member = (reader_id == reader_ref[:, lanes]).astype(f32)
        earlier = jnp.dot(member.astype(bf16), before, preferred_element_type=f32)
        rank = jnp.sum(member * (earlier + offset), axis=0, keepdims=True)
        offset = offset + jnp.sum(member, axis=1, keepdims=True)
        place = (slot_id == rank.astype(jnp.int32)).astype(f32).astype(bf16)
        vector = vector_ref[:, lanes] + KGRID
        vector = jnp.where(vector >= KGRID, vector - KGRID, vector)
        first = vector[0:1].astype(f32)
        plane = (vector[1:2] * KGRID + vector[2:3]).astype(f32)
        degen = degen_ref[:, lanes].astype(f32)
        digits = jnp.concatenate([member * first, member * plane, member * degen], axis=0)
        table = table + lax.dot_general(
            digits.astype(bf16), place, (((1,), (1,)), ((), ())), preferred_element_type=f32
        )
    degen = table[2 * READERS :]
    used = degen > 0.5
    residue = table[:READERS] * PLANE + table[READERS : 2 * READERS]
    residue_ref[...] = jnp.where(used, residue, -1.0).astype(jnp.int32)
    inverse_ref[...] = jnp.where(used, 1.0 / jnp.where(used, degen, 1.0), 0.0)

    rows, columns = kron_ref.shape
    row = lax.broadcasted_iota(jnp.int32, (rows, columns), 0)
    column = lax.broadcasted_iota(jnp.int32, (rows, columns), 1)
    pick = lax.broadcasted_iota(jnp.int32, (rows, 32), 0) >> 4
    pick = (pick == lax.broadcasted_iota(jnp.int32, (rows, 32), 1)).astype(f32).astype(bf16)
    phonon = jnp.dot(pick, phonon_ref[...].astype(f32).astype(bf16), preferred_element_type=f32)
    point = lax.broadcasted_iota(jnp.int32, (1, columns), 1) >> 4
    second = (point >= 6).astype(jnp.int32) + (point >= 12).astype(jnp.int32)
    third = point - 6 * second
    inner = phonon[:, 1:2] * second.astype(f32) + phonon[:, 2:3] * third.astype(f32)
    inner = inner - 6.0 * jnp.floor((inner + 0.5) * (1.0 / 6.0))
    half = jnp.float32(0.5)
    root = jnp.float32(0.8671875)
    cosine = jnp.where(inner > 3.5, inner - 6.0, inner)
    cosine = jnp.abs(cosine)
    cosine = jnp.where(
        cosine < 1.5,
        jnp.where(cosine < 0.5, 1.0, half),
        jnp.where(cosine < 2.5, -half, -1.0),
    )
    sine = jnp.where(inner > 3.5, -root, root)
    sine = jnp.where((inner < 0.5) | (jnp.abs(inner - 3.0) < 0.5), 0.0, sine)
    row_part = (row >> 3) & 1
    column_part = (column >> 3) & 1
    value = jnp.where(
        row_part == column_part, cosine, jnp.where(row_part == 0, sine, -sine)
    )
    kron_ref[...] = jnp.where((row & 7) == (column & 7), value, 0.0).astype(bf16)


def k_kernel(x_ref, plane_ref, residue_ref, out_ref, z_ref, y_ref, t_ref):
    f32, bf16 = jnp.float32, jnp.bfloat16
    width = x_ref.shape[2]
    scale = (KGRID**3) ** (-0.5)
    y_ref[...] = jnp.zeros_like(y_ref)
    for k in range(KGRID):
        z_ref[k] = jnp.dot(plane_ref[...], x_ref[k], preferred_element_type=f32)

    for tile in range(PLANE // 8):
        at = tile * 8
        real = [z_ref[k, at : at + 8, :] * scale for k in range(KGRID)]
        turned = [z_ref[k, PLANE + at : PLANE + at + 8, :] * scale for k in range(KGRID)]
        for r in range(KGRID):
            total = None
            for k in range(KGRID):
                angle = 2.0 * math.pi * ((r * k) % KGRID) / KGRID
                for weight, term in ((math.cos(angle), real[k]), (math.sin(angle), turned[k])):
                    if abs(weight) < 1e-9:
                        continue
                    term = term if abs(weight - 1.0) < 1e-9 else term * weight
                    total = term if total is None else total + term
            y_ref[r * PLANE + at : r * PLANE + at + 8, 0:width] = total
    t_ref[...] = y_ref[...].T.astype(bf16)

    row_id = lax.broadcasted_iota(jnp.int32, (ROWS, 256), 0)

    def pick(step, carry):
        left = residue_ref[pl.ds(2 * step, 1), :]
        right = residue_ref[pl.ds(2 * step + 1, 1), :]
        wanted = jnp.concatenate([left, right], axis=1)
        chosen = (row_id == wanted).astype(f32).astype(bf16)
        found = jnp.dot(t_ref[...], chosen, preferred_element_type=f32)[:width].astype(bf16)
        out_ref[pl.ds(2 * step, 1)] = found[None, :, :128]
        out_ref[pl.ds(2 * step + 1, 1)] = found[None, :, 128:]
        return carry

    lax.fori_loop(0, READERS // 2, pick, 0)


def q_kernel(groups, w_ref, kron_ref, inverse_ref, out_ref, s_ref):
    f32, bf16 = jnp.float32, jnp.bfloat16
    step = pl.program_id(0)

    @pl.when(step == 0)
    def _():
        pairs = w_ref.shape[1] // 2
        used = 2 * pairs
        s_ref[:, used - used % 8 :, :] = jnp.zeros((32, s_ref.shape[1] - used + used % 8, 128), f32)
        for source in range(32):
            point, half = source // 2, source % 2
            block = w_ref[source].astype(f32)
            for part in range(2):
                s_ref[2 * point + part, half * pairs : (half + 1) * pairs, :] = block[
                    part * pairs : (part + 1) * pairs
                ]

    inverse = inverse_ref[...] * 0.25
    for group in range(groups):
        at = pl.multiple_of((step * groups + group) * 8, 8)
        data = s_ref[:, pl.ds(at, 8), :].reshape(256, 128).astype(bf16)
        found = jnp.dot(kron_ref[...], data, preferred_element_type=f32) * inverse
        out_ref[:, group * 8 : group * 8 + 8, :] = found.reshape(64, 8, 128)


def per_device(coupling, rot_k, rot_kq, r_elec, degen, reader, r_phon):
    f32, bf16 = jnp.float32, jnp.bfloat16
    k_local = coupling.shape[1]
    total_r = r_elec.shape[0]
    shape = jax.ShapeDtypeStruct
    residue, inverse, kron = pl.pallas_call(
        table_kernel,
        out_shape=(
            shape((READERS, MOST), jnp.int32),
            shape((READERS, MOST), f32),
            shape((512, 256), bf16),
        ),
        in_specs=[VMEM] * 4,
        out_specs=(VMEM,) * 3,
        cost_estimate=pl.CostEstimate(flops=10**8, bytes_accessed=10**6, transcendentals=0),
        name="tables",
    )(reader.reshape(1, total_r), r_elec.T, degen.reshape(1, total_r), r_phon)
    my_inverse = lax.dynamic_slice_in_dim(inverse, lax.axis_index("ka"), 1)

    rotated = rotate(coupling, rot_k, rot_kq)
    pieces = rotated.reshape(k_local, 2, 16, 2, 50).transpose(2, 3, 0, 1, 4)
    pieces = pieces.reshape(16, 2, k_local, 100)
    pieces = lax.all_to_all(pieces, "pb", 0, 0, tiled=True)
    pieces = lax.all_to_all(pieces.reshape(32, k_local, 100), "ka", 0, 0, tiled=True)
    x = pieces.reshape(KGRID, PLANE, 100)
    turned = jnp.concatenate([x[:, :, 50:], -x[:, :, :50]], axis=2)
    x = jnp.concatenate([x, turned], axis=1)
    slots = pl.pallas_call(
        k_kernel,
        out_shape=shape((READERS, 100, MOST), bf16),
        in_specs=[VMEM] * 3,
        out_specs=VMEM,
        scratch_shapes=[
            pltpu.VMEM((KGRID, 2 * PLANE, 100), f32),
            pltpu.VMEM((ROWS, 128), f32),
            pltpu.VMEM((128, ROWS), bf16),
        ],
        compiler_params=pltpu.CompilerParams(vmem_limit_bytes=40 * 2**20),
        name="k_transform",
    )(x, jnp.asarray(plane_table()), residue)
    w = lax.all_to_all(slots, "ka", 0, 0, tiled=True)
    groups = 3
    out = pl.pallas_call(
        lambda *refs: q_kernel(groups, *refs),
        grid=(5,),
        out_shape=shape((64, 100, MOST), f32),
        in_specs=[
            pl.BlockSpec((32, 100, MOST), lambda i: (0, 0, 0)),
            pl.BlockSpec((512, 256), lambda i: (0, 0)),
            pl.BlockSpec((1, MOST), lambda i: (0, 0)),
        ],
        out_specs=pl.BlockSpec((64, 8 * groups, MOST), lambda i: (0, i, 0)),
        scratch_shapes=[pltpu.VMEM((32, 120, MOST), f32)],
        compiler_params=pltpu.CompilerParams(
            dimension_semantics=("arbitrary",), vmem_limit_bytes=40 * 2**20
        ),
        name="q_transform",
    )(w, kron, my_inverse)
    return out.reshape(32, 2, 100, MOST)


def solution(mesh):
    in_specs = (
        P("pb", "ka", None, None),
        P("ka", None, None),
        P("pb", "ka", None, None),
        P(),
        P(),
        P(),
        P(),
    )
    out_specs = P(None, None, "pb", "ka")
    return jax.shard_map(
        per_device, mesh=mesh, in_specs=in_specs, out_specs=out_specs, check_vma=False
    )
```

time: 322 us -> 116 us (0.36)
  the two profiles are of different devices: /device:TPU:1 before, /device:TPU:64 now
where the time goes in v1:
time: 116 us
  waiting for transfers between devices  37.5 us (32%)
  blocking collectives  21.5 us (19%)
  local copies, waits for them, and re-layouts  18.2 us (16%)
  starting transfers between devices  18 us (16%)
  Pallas kernels  12.7 us (11%)
  matrix products  6.9 us (6%)
    all_to_all x1, waiting for transfers between devices, per_device(): w = lax.all_to_all(slots, 'ka', 0, 0, tiled=True)  24.1 us
    all_to_all x1, blocking collectives, per_device(): pieces = lax.all_to_all(pieces, 'pb', 0, 0, tiled=True)  21.5 us
    all_to_all x1, waiting for transfers between devices, per_device(): lax.all_to_all(pieces.reshape(32, k_local, 100), 'ka', 0, 0, tiled=True)  13.4 us
    all_to_all x1, starting transfers between devices, per_device(): lax.all_to_all(pieces.reshape(32, k_local, 100), 'ka', 0, 0, tiled=True)  12.6 us
    pallas_call x1, Pallas kernels, per_device(): pl.pallas_call(k_kernel, out_shape=shape((READERS, 100, MOST), bf16), in_...  7.41 us
    dot_general x8, matrix products, product(): return jnp.einsum(spec, left, right, preferred_element_type=jnp.float32)  6.9 us
    all_to_all x1, starting transfers between devices, per_device(): w = lax.all_to_all(slots, 'ka', 0, 0, tiled=True)  5.45 us
    unnamed x22, local copies, waits for them, and re-layouts  3.58 us
  transfers between devices with their start and end apart: 2, of which 2 were waited for; matrix products, arithmetic and copies ran while one was open for 1% of the time, Pallas kernels for 3%

profile of v1, /device:TPU:64, one launch (start us, length us, event | category | flops | bytes accessed | tf_op | source)
XLA Modules:
  0.0 115.8 jit_solution(15473163858912075108)
XLA Ops:
  0.0 1.1 copy.59
  1.1 1.0 reshape.39
  2.2 1.0 reshape.40
  3.7 1.4 %fusion.6 = f32[54,40,40]{2,1,0:T(8,128)} fusion(bf16[54,2,40,40]{3,2,0,1:T(8,128)(2,1)S(1)} %reshape.39, bf16[54,2,40,40]{3,2,0,1:T(8,128)(2,1)S(1)} %reshape.40), kind=kOutput, calls=%fused_computation.18 | convolution fusion | flops 6912000 | bytes 1451520 | tf_op jit(solution)/shard_map/kab,kbn->kan/dot_general | solution.py:30
  5.1 1.3 %fusion = bf16[54,40,40]{2,1,0:T(8,128)(2,1)} fusion(f32[54,40,40]{2,1,0:T(8,128)S(1)} %fusion.7, bf16[54,2,40,40]{3,2,0,1:T(8,128)(2,1)S(1)} %reshape.39, bf16[54,2,40,40]{3,2,0,1:T(8,128)(2,1)S(1)} %reshape.40), kind=kOutput, calls=%fused_computation.4 | convolution fusion | flops 7084800 | bytes 2384640 | tf_op jit(solution)/shard_map/kab,kbn->kan/dot_general | solution.py:30
  6.4 0.8 copy.61
  7.2 2.0 %reshape.41 = bf16[54,2,40,40]{3,2,0,1:T(8,128)(2,1)S(1)} reshape(bf16[1,54,2,1600]{3,1,2,0:T(8,128)(2,1)} %copy.61) | data formatting | bytes 691200 | tf_op jit(solution)/shard_map/reshape | solution.py:37
  9.2 1.7 %fusion.1 = bf16[54,40,40]{2,1,0:T(8,128)(2,1)S(1)} fusion(f32[54,40,40]{2,1,0:T(8,128)} %fusion.6, bf16[54,2,40,40]{3,2,0,1:T(8,128)(2,1)S(1)} %reshape.40, bf16[54,2,40,40]{3,2,0,1:T(8,128)(2,1)S(1)} %reshape.39), kind=kOutput, calls=%fused_computation.5 | convolution fusion | flops 7084800 | bytes 1624320 | tf_op jit(solution)/shard_map/kab,kbn->kan/dot_general | solution.py:30
  12.5 1.2 %copy.64 = bf16[54,40,40]{0,2,1:T(8,128)(2,1)} copy(bf16[54,40,40]{1,2,0:T(8,128)(2,1)S(1)} %fusion.5) | data formatting | bytes 345600 | tf_op jit(solution)/shard_map/add | solution.py:44
  13.7 1.9 %stack.9 = bf16[54,1,16,2,50]{0,4,3,2,1:T(8,128)(2,1)} reshape(bf16[54,40,40]{0,2,1:T(8,128)(2,1)} %copy.64) | data formatting | bytes 345600 | tf_op jit(solution)/shard_map/stack | solution.py:46
  17.3 1.0 copy.78
  18.7 21.5 %all_to_all.15 = bf16[16,2,54,100]{3,1,2,0:T(2,128)(2,1)S(1)} all-to-all(bf16[16,2,54,100]{3,1,2,0:T(2,128)(2,1)S(1)} %reshape.48), channel_id=1, replica_groups=mesh['pb'=16,'ka'=32] {'pb'}, dimensions={0} | all-to-all | bytes 691200 | tf_op jit(solution)/shard_map/all_to_all | solution.py:198
  40.6 0.9 copy.71
  41.5 12.6 %all-to-all-start.1 = ((bf16[32,54,100]{2,1,0:T(8,128)(2,1)}), bf16[32,54,100]{2,1,0:T(8,128)(2,1)S(1)}, u32[]{:S(2)}, u32[]{:S(2)}) async-start(bf16[32,54,100]{2,1,0:T(8,128)(2,1)} %copy.71), calls=%async_computation.1 | async-start | bytes 917504 | tf_op jit(solution)/shard_map/all_to_all | solution.py:199
  54.1 0.7 copy.72.phonon_ref
  54.8 3.0 %tables.1 = (s32[32,128]{1,0:T(8,128)}, f32[32,128]{1,0:T(8,128)}, bf16[512,256]{1,0:T(8,128)(2,1)}) custom-call(s32[1,2048]{1,0:T(1,128)} %bitcast.54, s32[3,2048]{1,0:T(4,128)} %bitcast.53, s32[1,2048]{1,0:T(1,128)} %bitcast.55, s32[32,3]{1,0:T(8,128)} %copy.72.phonon_ref), custom_call_target="tpu_custom_call" | custom-call | flops 100000000 | bytes 1000000 | tf_op jit(solution)/shard_map/tables/pallas_call | solution.py:181
  57.8 13.4 %all-to-all-done.1 = bf16[32,54,100]{2,1,0:T(8,128)(2,1)S(1)} async-done(((bf16[32,54,100]{2,1,0:T(8,128)(2,1)}), bf16[32,54,100]{2,1,0:T(8,128)(2,1)S(1)}, u32[]{:S(2)}, u32[]{:S(2)}) %all-to-all-start.1) | async-done | bytes 345632 | tf_op jit(solution)/shard_map/all_to_all | solution.py:199
  71.9 0.6 copy-done.1
  72.5 7.4 %k_transform.1 = bf16[32,100,128]{2,1,0:T(8,128)(2,1)} custom-call(bf16[12,288,100]{2,1,0:T(8,128)(2,1)S(1)} %maximum_maximum_fusion.x_ref, bf16[288,288]{1,0:T(8,128)(2,1)S(1)} %copy-done.1, s32[32,128]{1,0:T(8,128)S(1)} %copy-done.2), custom_call_target="tpu_custom_call" | custom-call | tf_op jit(solution)/shard_map/k_transform/pallas_call | solution.py:203
  79.9 5.5 %all-to-all-start.2 = ((bf16[32,100,128]{2,1,0:T(8,128)(2,1)}), bf16[32,100,128]{2,1,0:T(8,128)(2,1)S(1)}, u32[]{:S(2)}, u32[]{:S(2)}) async-start(bf16[32,100,128]{2,1,0:T(8,128)(2,1)} %k_transform.1), calls=%async_computation.2 | async-start | bytes 1703936 | tf_op jit(solution)/shard_map/all_to_all | solution.py:216
  85.3 0.7 constant_dynamic-slice_fusion.refs_2_
  86.0 24.1 %all-to-all-done.2.refs_0_ = bf16[32,100,128]{2,1,0:T(8,128)(2,1)S(1)} async-done(((bf16[32,100,128]{2,1,0:T(8,128)(2,1)}), bf16[32,100,128]{2,1,0:T(8,128)(2,1)S(1)}, u32[]{:S(2)}, u32[]{:S(2)}) %all-to-all-start.2) | async-done | bytes 819232 | tf_op jit(solution)/shard_map/all_to_all | solution.py:216
  110.1 2.3 %q_transform.1 = f32[64,100,128]{2,1,0:T(8,128)S(1)} custom-call(bf16[32,100,128]{2,1,0:T(8,128)(2,1)S(1)} %all-to-all-done.2.refs_0_, bf16[512,256]{1,0:T(8,128)(2,1)S(1)} %copy-done, f32[1,128]{1,0:T(1,128)S(1)} %constant_dynamic-slice_fusion.refs_2_), custom_call_target="tpu_custom_call" | custom-call | tf_op jit(solution)/shard_map/q_transform/pallas_call | solution.py:218
  112.4 3.4 %copy.73 = f32[32,2,100,128]{3,1,2,0:T(2,128)} copy(f32[32,2,100,128]{3,2,1,0:T(8,128)S(1)} %bitcast.51) | data formatting | bytes 6553600 | tf_op jit(solution)/shard_map/reshape | solution.py:234
  (31 shorter events, 5.1 us)
Async XLA Ops:
  0.0 2.1 %copy-start.6 = (bf16[54,2,1600]{2,1,0:T(2,128)(2,1)S(1)}, bf16[54,2,1600]{2,1,0:T(2,128)(2,1)}, u32[]{:S(2)}) copy-start(bf16[54,2,1600]{2,1,0:T(2,128)(2,1)} %param.9) | copy-start | bytes 1036804
  5.1 1.3 %copy-start.7 = (bf16[1,54,2,1600]{3,2,1,0:T(2,128)(2,1)S(1)}, bf16[1,54,2,1600]{3,2,1,0:T(2,128)(2,1)}, u32[]{:S(2)}) copy-start(bf16[1,54,2,1600]{3,2,1,0:T(2,128)(2,1)} %param.10) | copy-start | bytes 1036804
  9.2 1.8 %copy-start.3 = (bf16[54,40,40]{2,1,0:T(8,128)(2,1)S(1)}, bf16[54,40,40]{2,1,0:T(8,128)(2,1)}, u32[]{:S(2)}) copy-start(bf16[54,40,40]{2,1,0:T(8,128)(2,1)} %fusion) | copy-start | bytes 518404
  12.5 3.1 %copy-start.4 = (bf16[54,40,40]{2,1,0:T(8,128)(2,1)S(1)}, bf16[54,40,40]{2,1,0:T(8,128)(2,1)}, u32[]{:S(2)}) copy-start(bf16[54,40,40]{2,1,0:T(8,128)(2,1)} %fusion) | copy-start | bytes 518404
  16.1 1.0 copy-start.5
  40.5 13.6 %copy-start.8 = (s32[32,3]{0,1:T(4,128)S(1)}, s32[32,3]{0,1:T(4,128)}, u32[]{:S(2)}) copy-start(s32[32,3]{0,1:T(4,128)} %param.14) | copy-start | bytes 1156
  41.5 29.7 %all-to-all-start.1 = ((bf16[32,54,100]{2,1,0:T(8,128)(2,1)}), bf16[32,54,100]{2,1,0:T(8,128)(2,1)S(1)}, u32[]{:S(2)}, u32[]{:S(2)}) async-start(bf16[32,54,100]{2,1,0:T(8,128)(2,1)} %copy.71), calls=%async_computation.1 | async-start | bytes 917504 | tf_op jit(solution)/shard_map/all_to_all | solution.py:199
  71.5 0.9 copy-start.1
  71.5 0.9 copy-start.2
  79.9 30.2 %copy-start = (bf16[512,256]{1,0:T(8,128)(2,1)S(1)}, bf16[512,256]{1,0:T(8,128)(2,1)}, u32[]{:S(2)}) copy-start(bf16[512,256]{1,0:T(8,128)(2,1)} %get-tuple-element.9.refs_1_) | copy-start | bytes 786436
  79.9 30.2 %all-to-all-start.2 = ((bf16[32,100,128]{2,1,0:T(8,128)(2,1)}), bf16[32,100,128]{2,1,0:T(8,128)(2,1)S(1)}, u32[]{:S(2)}, u32[]{:S(2)}) async-start(bf16[32,100,128]{2,1,0:T(8,128)(2,1)} %k_transform.1), calls=%async_computation.2 | async-start | bytes 1703936 | tf_op jit(solution)/shard_map/all_to_all | solution.py:216

commit v2 on v1

--- a/solution.py
+++ b/solution.py
@@ -101,12 +101,12 @@
     )
     sine = jnp.where(inner > 3.5, -root, root)
     sine = jnp.where((inner < 0.5) | (jnp.abs(inner - 3.0) < 0.5), 0.0, sine)
-    row_part = (row >> 3) & 1
+    row_part = row & 1
     column_part = (column >> 3) & 1
     value = jnp.where(
         row_part == column_part, cosine, jnp.where(row_part == 0, sine, -sine)
     )
-    kron_ref[...] = jnp.where((row & 7) == (column & 7), value, 0.0).astype(bf16)
+    kron_ref[...] = jnp.where(((row >> 1) & 7) == (column & 7), value, 0.0).astype(bf16)
 
 
 def k_kernel(x_ref, plane_ref, residue_ref, out_ref, z_ref, y_ref, t_ref):
@@ -140,12 +140,110 @@
         right = residue_ref[pl.ds(2 * step + 1, 1), :]
         wanted = jnp.concatenate([left, right], axis=1)
         chosen = (row_id == wanted).astype(f32).astype(bf16)
-        found = jnp.dot(t_ref[...], chosen, preferred_element_type=f32)[:width].astype(bf16)
+        found = jnp.dot(t_ref[...], chosen, preferred_element_type=f32)[:112].astype(bf16)
         out_ref[pl.ds(2 * step, 1)] = found[None, :, :128]
         out_ref[pl.ds(2 * step + 1, 1)] = found[None, :, 128:]
         return carry
 
     lax.fori_loop(0, READERS // 2, pick, 0)
+
+
+def exchange_kernel(rotated, x_ref, out_ref, send_sem, recv_sem, self_sem):
+    pb, ka = lax.axis_index("pb"), lax.axis_index("ka")
+    source = lax.rem(ka // 2 + 16 - pb, 16) if rotated else pb
+
+    def target(step):
+        if not rotated:
+            to = lax.rem(ka + step, 32)
+            return to, pb, to
+        to = lax.rem(pb + step // 2, 16)
+        half = step % 2
+        return 2 * to + half, to, lax.rem(2 * (pb + to) + half, 32)
+
+    def is_self(to_pb, to_ka):
+        return jnp.logical_and(to_pb == pb, to_ka == ka)
+
+    def remote(step, row, landing, device):
+        return pltpu.make_async_remote_copy(
+            src_ref=x_ref.at[row],
+            dst_ref=out_ref.at[landing],
+            send_sem=send_sem.at[step],
+            recv_sem=recv_sem.at[landing],
+            device_id=device,
+            device_id_type=pl.DeviceIdType.MESH,
+        )
+
+    barrier = pltpu.get_barrier_semaphore()
+
+    def greet(other, carry):
+        @pl.when(jnp.logical_not(is_self(source, other)))
+        def _():
+            pl.semaphore_signal(
+                barrier, inc=1, device_id=(source, other), device_id_type=pl.DeviceIdType.MESH
+            )
+
+        return carry
+
+    lax.fori_loop(0, 32, greet, 0)
+    pl.semaphore_wait(barrier, 31 if not rotated else jnp.where(source == pb, 31, 32))
+
+    def send(step, carry):
+        row, to_pb, to_ka = target(step)
+        own = is_self(to_pb, to_ka)
+
+        @pl.when(own)
+        def _():
+            pltpu.make_async_copy(x_ref.at[row], out_ref.at[ka], self_sem).start()
+
+        @pl.when(jnp.logical_not(own))
+        def _():
+            remote(step, row, ka, (to_pb, to_ka)).start()
+
+        return carry
+
+    lax.fori_loop(0, 32, send, 0)
+
+    def receive(other, carry):
+        own = is_self(source, other)
+
+        @pl.when(own)
+        def _():
+            pltpu.make_async_copy(x_ref.at[0], out_ref.at[other], self_sem).wait()
+
+        @pl.when(jnp.logical_not(own))
+        def _():
+            remote(0, 0, other, (source, other)).wait_recv()
+
+        return carry
+
+    lax.fori_loop(0, 32, receive, 0)
+
+    def sent(step, carry):
+        row, to_pb, to_ka = target(step)
+
+        @pl.when(jnp.logical_not(is_self(to_pb, to_ka)))
+        def _():
+            remote(step, row, ka, (to_pb, to_ka)).wait_send()
+
+        return carry
+
+    lax.fori_loop(0, 32, sent, 0)
+
+
+def exchange(x, rotated, number, name):
+    return pl.pallas_call(
+        lambda *refs: exchange_kernel(rotated, *refs),
+        out_shape=jax.ShapeDtypeStruct(x.shape, x.dtype),
+        in_specs=[VMEM],
+        out_specs=VMEM,
+        scratch_shapes=[
+            pltpu.SemaphoreType.DMA((32,)),
+            pltpu.SemaphoreType.DMA((32,)),
+            pltpu.SemaphoreType.DMA,
+        ],
+        compiler_params=pltpu.CompilerParams(collective_id=number, has_side_effects=True),
+        name=name,
+    )(x)
 
 
 def q_kernel(groups, w_ref, kron_ref, inverse_ref, out_ref, s_ref):
@@ -154,12 +252,13 @@
 
     @pl.when(step == 0)
     def _():
-        pairs = w_ref.shape[1] // 2
+        pairs = 50
+        shift = 2 * lax.axis_index("pb")
         used = 2 * pairs
         s_ref[:, used - used % 8 :, :] = jnp.zeros((32, s_ref.shape[1] - used + used % 8, 128), f32)
         for source in range(32):
             point, half = source // 2, source % 2
-            block = w_ref[source].astype(f32)
+            block = w_ref[lax.rem(source + shift, 32)].astype(f32)
             for part in range(2):
                 s_ref[2 * point + part, half * pairs : (half + 1) * pairs, :] = block[
                     part * pairs : (part + 1) * pairs
@@ -170,7 +269,7 @@
         at = pl.multiple_of((step * groups + group) * 8, 8)
         data = s_ref[:, pl.ds(at, 8), :].reshape(256, 128).astype(bf16)
         found = jnp.dot(kron_ref[...], data, preferred_element_type=f32) * inverse
-        out_ref[:, group * 8 : group * 8 + 8, :] = found.reshape(64, 8, 128)
+        out_ref[:, group * 16 : group * 16 + 16, :] = found.reshape(32, 16, 128)
 
 
 def per_device(coupling, rot_k, rot_kq, r_elec, degen, reader, r_phon):
@@ -194,15 +293,15 @@
 
     rotated = rotate(coupling, rot_k, rot_kq)
     pieces = rotated.reshape(k_local, 2, 16, 2, 50).transpose(2, 3, 0, 1, 4)
-    pieces = pieces.reshape(16, 2, k_local, 100)
-    pieces = lax.all_to_all(pieces, "pb", 0, 0, tiled=True)
-    pieces = lax.all_to_all(pieces.reshape(32, k_local, 100), "ka", 0, 0, tiled=True)
+    pieces = pieces.reshape(32, k_local, 100)
+    pieces = jnp.pad(pieces, ((0, 0), (0, 64 - k_local), (0, 28)))
+    pieces = exchange(pieces, True, 1, "to_pairs")[:, :k_local, :100]
     x = pieces.reshape(KGRID, PLANE, 100)
     turned = jnp.concatenate([x[:, :, 50:], -x[:, :, :50]], axis=2)
     x = jnp.concatenate([x, turned], axis=1)
     slots = pl.pallas_call(
         k_kernel,
-        out_shape=shape((READERS, 100, MOST), bf16),
+        out_shape=shape((READERS, 112, MOST), bf16),
         in_specs=[VMEM] * 3,
         out_specs=VMEM,
         scratch_shapes=[
@@ -213,25 +312,25 @@
         compiler_params=pltpu.CompilerParams(vmem_limit_bytes=40 * 2**20),
         name="k_transform",
     )(x, jnp.asarray(plane_table()), residue)
-    w = lax.all_to_all(slots, "ka", 0, 0, tiled=True)
+    w = exchange(slots, False, 2, "to_readers")
     groups = 3
     out = pl.pallas_call(
         lambda *refs: q_kernel(groups, *refs),
         grid=(5,),
-        out_shape=shape((64, 100, MOST), f32),
+        out_shape=shape((32, 200, MOST), f32),
         in_specs=[
-            pl.BlockSpec((32, 100, MOST), lambda i: (0, 0, 0)),
+            pl.BlockSpec((32, 112, MOST), lambda i: (0, 0, 0)),
             pl.BlockSpec((512, 256), lambda i: (0, 0)),
             pl.BlockSpec((1, MOST), lambda i: (0, 0)),
         ],
-        out_specs=pl.BlockSpec((64, 8 * groups, MOST), lambda i: (0, i, 0)),
+        out_specs=pl.BlockSpec((32, 16 * groups, MOST), lambda i: (0, i, 0)),
         scratch_shapes=[pltpu.VMEM((32, 120, MOST), f32)],
         compiler_params=pltpu.CompilerParams(
             dimension_semantics=("arbitrary",), vmem_limit_bytes=40 * 2**20
         ),
         name="q_transform",
     )(w, kron, my_inverse)
-    return out.reshape(32, 2, 100, MOST)
+    return out.reshape(32, 100, 2, MOST).transpose(0, 2, 1, 3)
 
 
 def solution(mesh):

time: 116 us -> 105 us (0.905)
  the two profiles are of different devices: /device:TPU:64 before, /device:TPU:1 now
where the time goes in v2:
time: 105 us
  Pallas kernels  80.6 us (77%)
  local copies, waits for them, and re-layouts  17.3 us (16%)
  matrix products  5.64 us (5%)
    pallas_call x2, Pallas kernels, exchange(): pl.pallas_call(lambda *refs: exchange_kernel(rotated, *refs), out_shape=j...  67.5 us
    unnamed x26, local copies, waits for them, and re-layouts  7.52 us
    pallas_call x1, Pallas kernels, per_device(): pl.pallas_call(k_kernel, out_shape=shape((READERS, 112, MOST), bf16), in_...  6.5 us
    dot_general x8, matrix products, product(): return jnp.einsum(spec, left, right, preferred_element_type=jnp.float32)  5.64 us
    pallas_call x1, Pallas kernels, per_device(): pl.pallas_call(lambda *refs: q_kernel(groups, *refs), grid=(5,), out_shap...  3.68 us
    pallas_call x1, Pallas kernels, per_device(): pl.pallas_call(table_kernel, out_shape=(shape((READERS, MOST), jnp.int32)...  2.96 us

profile of v2, /device:TPU:1, one launch (start us, length us, event | category | flops | bytes accessed | tf_op | source)
XLA Modules:
  0.0 104.5 jit_solution(16721468110342745251)
XLA Ops:
  0.0 1.1 %copy.17 = bf16[1,54,2,1600]{3,1,2,0:T(8,128)(2,1)S(1)} copy(bf16[1,54,2,1600]{3,2,1,0:T(2,128)(2,1)} %param.8) | data formatting | bytes 691200 | tf_op args[0]
  1.1 1.0 reshape.36
  2.2 1.0 reshape.37
  3.7 1.3 %fusion = bf16[54,40,40]{2,1,0:T(8,128)(2,1)} fusion(f32[54,40,40]{2,1,0:T(8,128)S(1)} %fusion.7, bf16[54,2,40,40]{3,2,0,1:T(8,128)(2,1)S(1)} %reshape.36, bf16[54,2,40,40]{3,2,0,1:T(8,128)(2,1)S(1)} %reshape.37), kind=kOutput, calls=%fused_computation.4 | convolution fusion | flops 7084800 | bytes 2384640 | tf_op jit(solution)/shard_map/kab,kbn->kan/dot_general | solution.py:30
  4.9 0.8 copy.19
  5.7 2.0 %reshape.38 = bf16[54,2,40,40]{3,2,0,1:T(8,128)(2,1)S(1)} reshape(bf16[1,54,2,1600]{3,1,2,0:T(8,128)(2,1)} %copy.19) | data formatting | bytes 691200 | tf_op jit(solution)/shard_map/reshape | solution.py:37
  7.7 1.5 %fusion.9 = f32[54,40,40]{2,1,0:T(8,128)S(1)} fusion(bf16[54,40,40]{2,1,0:T(8,128)(2,1)} %fusion, bf16[54,2,40,40]{3,2,0,1:T(8,128)(2,1)S(1)} %reshape.38), kind=kOutput, calls=%fused_computation.21 | convolution fusion | flops 6912000 | bytes 1071360 | tf_op jit(solution)/shard_map/kam,kan->kmn/dot_general | solution.py:30
  10.2 0.8 copy-done.6
  11.0 0.5 fusion.5
  13.1 0.6 copy-done.5
  13.6 0.5 fusion.4
  15.0 1.2 %copy.33 = bf16[16,2,54,2,50]{4,3,2,1,0:T(2,128)(2,1)S(1)} copy(bf16[16,2,54,2,50]{2,4,1,0,3:T(8,128)(2,1)S(1)} %maximum_bitcast_fusion) | data formatting | bytes 691200 | tf_op jit(solution)/shard_map/reshape | solution.py:296
  16.6 0.9 pad.4.refs_0_
  17.6 31.1 %to_pairs.1 = bf16[32,64,128]{2,1,0:T(8,128)(2,1)} custom-call(bf16[32,64,128]{2,1,0:T(8,128)(2,1)} %pad.4.refs_0_), custom_call_target="tpu_custom_call" | custom-call | tf_op jit(solution)/shard_map/to_pairs/pallas_call | solution.py:234
  48.7 1.1 %slice.39 = bf16[32,54,100]{2,1,0:T(8,128)(2,1)S(1)} slice(bf16[32,64,128]{2,1,0:T(8,128)(2,1)} %to_pairs.1), slice={[0:32], [0:54], [0:100]} | slice | bytes 691200 | tf_op jit(solution)/shard_map/slice | solution.py:298
  50.8 0.7 copy.28.phonon_ref
  51.5 3.0 %tables.1 = (s32[32,128]{1,0:T(8,128)}, f32[32,128]{1,0:T(8,128)}, bf16[512,256]{1,0:T(8,128)(2,1)}) custom-call(s32[1,2048]{1,0:T(1,128)} %bitcast.51, s32[3,2048]{1,0:T(4,128)} %bitcast.50, s32[1,2048]{1,0:T(1,128)} %bitcast.52, s32[32,3]{1,0:T(8,128)} %copy.28.phonon_ref), custom_call_target="tpu_custom_call" | custom-call | flops 100000000 | bytes 1000000 | tf_op jit(solution)/shard_map/tables/pallas_call | solution.py:280
  54.4 0.7 copy-done.4
  55.1 6.5 %k_transform.1.refs_0_ = bf16[32,112,128]{2,1,0:T(8,128)(2,1)S(1)} custom-call(bf16[12,288,100]{2,1,0:T(8,128)(2,1)S(1)} %maximum_maximum_fusion.x_ref, bf16[288,288]{1,0:T(8,128)(2,1)S(1)} %copy-done.3, s32[32,128]{1,0:T(8,128)S(1)} %copy-done.4), custom_call_target="tpu_custom_call" | custom-call | tf_op jit(solution)/shard_map/k_transform/pallas_call | solution.py:302
  61.7 0.9 copy-done.1
  62.6 36.4 %to_readers.1.refs_0_ = bf16[32,112,128]{2,1,0:T(8,128)(2,1)} custom-call(bf16[32,112,128]{2,1,0:T(8,128)(2,1)} %copy-done.1), custom_call_target="tpu_custom_call" | custom-call | tf_op jit(solution)/shard_map/to_readers/pallas_call | solution.py:234
  99.0 0.7 constant_dynamic-slice_fusion.refs_2_
  99.7 1.2 %copy-done = bf16[32,112,128]{2,1,0:T(8,128)(2,1)S(1)} copy-done((bf16[32,112,128]{2,1,0:T(8,128)(2,1)S(1)}, bf16[32,112,128]{2,1,0:T(8,128)(2,1)}, u32[]{:S(2)}) %copy-start) | copy-done | bytes 917528
  100.9 3.7 %q_transform.1 = f32[32,200,128]{2,1,0:T(8,128)} custom-call(bf16[32,112,128]{2,1,0:T(8,128)(2,1)S(1)} %copy-done, bf16[512,256]{1,0:T(8,128)(2,1)S(1)} %copy-done.2, f32[1,128]{1,0:T(1,128)S(1)} %constant_dynamic-slice_fusion.refs_2_), custom_call_target="tpu_custom_call" | custom-call | tf_op jit(solution)/shard_map/q_transform/pallas_call | solution.py:317
  (31 shorter events, 5.2 us)
Async XLA Ops:
  0.0 2.1 %copy-start.8 = (bf16[54,2,1600]{2,1,0:T(2,128)(2,1)S(1)}, bf16[54,2,1600]{2,1,0:T(2,128)(2,1)}, u32[]{:S(2)}) copy-start(bf16[54,2,1600]{2,1,0:T(2,128)(2,1)} %param.9) | copy-start | bytes 1036804
  3.7 1.3 %copy-start.9 = (bf16[1,54,2,1600]{3,2,1,0:T(2,128)(2,1)S(1)}, bf16[1,54,2,1600]{3,2,1,0:T(2,128)(2,1)}, u32[]{:S(2)}) copy-start(bf16[1,54,2,1600]{3,2,1,0:T(2,128)(2,1)} %param.10) | copy-start | bytes 1036804
  10.2 0.8 copy-start.6
  11.5 1.1 %copy-start.7 = (bf16[54,40,40]{2,1,0:T(8,128)(2,1)S(1)}, bf16[54,40,40]{2,1,0:T(8,128)(2,1)}, u32[]{:S(2)}) copy-start(bf16[54,40,40]{2,1,0:T(8,128)(2,1)} %copy-done.6) | copy-start | bytes 518404
  12.6 1.1 %copy-start.5 = (bf16[54,40,40]{2,1,0:T(8,128)(2,1)S(1)}, bf16[54,40,40]{2,1,0:T(8,128)(2,1)}, u32[]{:S(2)}) copy-start(bf16[54,40,40]{2,1,0:T(8,128)(2,1)} %fusion) | copy-start | bytes 518404
  50.1 0.7 copy-start.10
  50.1 4.3 %copy-start.3 = (bf16[288,288]{1,0:T(8,128)(2,1)S(1)}, bf16[288,288]{1,0:T(8,128)(2,1)}, u32[]{:S(2)}) copy-start(bf16[288,288]{1,0:T(8,128)(2,1)} %constant.12.clone.plane_ref) | copy-start | bytes 497668
  54.4 0.7 copy-start.4
  61.7 0.9 copy-start.1
  62.6 37.1 %copy-start.2 = (bf16[512,256]{1,0:T(8,128)(2,1)S(1)}, bf16[512,256]{1,0:T(8,128)(2,1)}, u32[]{:S(2)}) copy-start(bf16[512,256]{1,0:T(8,128)(2,1)} %get-tuple-element.9.refs_1_) | copy-start | bytes 786436
  99.7 1.2 %copy-start = (bf16[32,112,128]{2,1,0:T(8,128)(2,1)S(1)}, bf16[32,112,128]{2,1,0:T(8,128)(2,1)}, u32[]{:S(2)}) copy-start(bf16[32,112,128]{2,1,0:T(8,128)(2,1)} %to_readers.1.refs_0_) | copy-start | bytes 2752516

commit v3 on v2

--- a/solution.py
+++ b/solution.py
@@ -140,7 +140,7 @@
         right = residue_ref[pl.ds(2 * step + 1, 1), :]
         wanted = jnp.concatenate([left, right], axis=1)
         chosen = (row_id == wanted).astype(f32).astype(bf16)
-        found = jnp.dot(t_ref[...], chosen, preferred_element_type=f32)[:112].astype(bf16)
+        found = jnp.dot(t_ref[...], chosen, preferred_element_type=f32)[:104].astype(bf16)
         out_ref[pl.ds(2 * step, 1)] = found[None, :, :128]
         out_ref[pl.ds(2 * step + 1, 1)] = found[None, :, 128:]
         return carry
@@ -154,9 +154,10 @@
 
     def target(step):
         if not rotated:
-            to = lax.rem(ka + step, 32)
+            shift = lax.rem(13 * step, 32)
+            to = lax.rem(ka // 8 + shift // 8, 4) * 8 + lax.rem(ka + shift, 8)
             return to, pb, to
-        to = lax.rem(pb + step // 2, 16)
+        to = lax.rem(pb + 5 * (step // 2), 16)
         half = step % 2
         return 2 * to + half, to, lax.rem(2 * (pb + to) + half, 32)
 
@@ -264,7 +265,7 @@
                     part * pairs : (part + 1) * pairs
                 ]
 
-    inverse = inverse_ref[...] * 0.25
+    inverse = inverse_ref[pl.ds(lax.axis_index("ka"), 1), :] * 0.25
     for group in range(groups):
         at = pl.multiple_of((step * groups + group) * 8, 8)
         data = s_ref[:, pl.ds(at, 8), :].reshape(256, 128).astype(bf16)
@@ -289,19 +290,18 @@
         cost_estimate=pl.CostEstimate(flops=10**8, bytes_accessed=10**6, transcendentals=0),
         name="tables",
     )(reader.reshape(1, total_r), r_elec.T, degen.reshape(1, total_r), r_phon)
-    my_inverse = lax.dynamic_slice_in_dim(inverse, lax.axis_index("ka"), 1)
 
     rotated = rotate(coupling, rot_k, rot_kq)
     pieces = rotated.reshape(k_local, 2, 16, 2, 50).transpose(2, 3, 0, 1, 4)
     pieces = pieces.reshape(32, k_local, 100)
-    pieces = jnp.pad(pieces, ((0, 0), (0, 64 - k_local), (0, 28)))
+    pieces = jnp.pad(pieces, ((0, 0), (0, 56 - k_local), (0, 28)))
     pieces = exchange(pieces, True, 1, "to_pairs")[:, :k_local, :100]
     x = pieces.reshape(KGRID, PLANE, 100)
     turned = jnp.concatenate([x[:, :, 50:], -x[:, :, :50]], axis=2)
     x = jnp.concatenate([x, turned], axis=1)
     slots = pl.pallas_call(
         k_kernel,
-        out_shape=shape((READERS, 112, MOST), bf16),
+        out_shape=shape((READERS, 104, MOST), bf16),
         in_specs=[VMEM] * 3,
         out_specs=VMEM,
         scratch_shapes=[
@@ -319,9 +319,9 @@
         grid=(5,),
         out_shape=shape((32, 200, MOST), f32),
         in_specs=[
-            pl.BlockSpec((32, 112, MOST), lambda i: (0, 0, 0)),
+            pl.BlockSpec((32, 104, MOST), lambda i: (0, 0, 0)),
             pl.BlockSpec((512, 256), lambda i: (0, 0)),
-            pl.BlockSpec((1, MOST), lambda i: (0, 0)),
+            pl.BlockSpec((READERS, MOST), lambda i: (0, 0)),
         ],
         out_specs=pl.BlockSpec((32, 16 * groups, MOST), lambda i: (0, i, 0)),
         scratch_shapes=[pltpu.VMEM((32, 120, MOST), f32)],
@@ -329,7 +329,7 @@
             dimension_semantics=("arbitrary",), vmem_limit_bytes=40 * 2**20
         ),
         name="q_transform",
-    )(w, kron, my_inverse)
+    )(w, kron, inverse)
     return out.reshape(32, 100, 2, MOST).transpose(0, 2, 1, 3)
 
 

time: 105 us -> 102 us (0.971)
  Pallas kernels: 80.6 us -> 78.1 us
    pallas_call x2, Pallas kernels: 67.5 us -> 64.9 us  [exchange(): pl.pallas_call(lambda *refs: exchange_kernel(rotated, *refs), out_shape=j...]
    slice x1 -> x0, local copies, waits for them, and re-layouts: 1.06 us -> none  [per_device(): pieces = exchange(pieces, True, 1, 'to_pairs')[:, :k_local, :100]]
    unnamed x26 -> x28, local copies, waits for them, and re-layouts: 7.52 us -> 7.47 us
where the time goes in v3:
time: 102 us; the launch traced here: 101 us
  Pallas kernels  78.1 us (77%)
  local copies, waits for them, and re-layouts  16.4 us (16%)
  matrix products  5.63 us (6%)
    pallas_call x2, Pallas kernels, exchange(): pl.pallas_call(lambda *refs: exchange_kernel(rotated, *refs), out_shape=j...  64.9 us
    unnamed x28, local copies, waits for them, and re-layouts  7.47 us
    pallas_call x1, Pallas kernels, per_device(): pl.pallas_call(k_kernel, out_shape=shape((READERS, 104, MOST), bf16), in_...  6.5 us
    dot_general x8, matrix products, product(): return jnp.einsum(spec, left, right, preferred_element_type=jnp.float32)  5.63 us
    pallas_call x1, Pallas kernels, per_device(): pl.pallas_call(lambda *refs: q_kernel(groups, *refs), grid=(5,), out_shap...  3.68 us
    pallas_call x1, Pallas kernels, per_device(): pl.pallas_call(table_kernel, out_shape=(shape((READERS, MOST), jnp.int32)...  2.99 us

profile of v3, /device:TPU:1, one launch (start us, length us, event | category | flops | bytes accessed | tf_op | source)
XLA Modules:
  0.0 101.2 jit_solution(9290493375021570804)
XLA Ops:
  0.0 1.1 %copy.17 = bf16[1,54,2,1600]{3,1,2,0:T(8,128)(2,1)S(1)} copy(bf16[1,54,2,1600]{3,2,1,0:T(2,128)(2,1)} %param.8) | data formatting | bytes 691200 | tf_op args[0]
  1.1 1.0 %reshape.36 = bf16[54,2,40,40]{3,2,0,1:T(8,128)(2,1)S(1)} reshape(bf16[1,54,2,1600]{3,1,2,0:T(8,128)(2,1)S(1)} %copy.17) | data formatting | bytes 691200 | tf_op jit(solution)/shard_map/reshape | solution.py:35
  2.2 1.0 %reshape.37 = bf16[54,2,40,40]{3,2,0,1:T(8,128)(2,1)S(1)} reshape(bf16[54,2,1600]{2,0,1:T(8,128)(2,1)S(1)} %copy.18) | data formatting | bytes 691200 | tf_op jit(solution)/shard_map/reshape | solution.py:36
  3.7 1.2 %fusion = bf16[54,40,40]{2,1,0:T(8,128)(2,1)} fusion(f32[54,40,40]{2,1,0:T(8,128)S(1)} %fusion.7, bf16[54,2,40,40]{3,2,0,1:T(8,128)(2,1)S(1)} %reshape.36, bf16[54,2,40,40]{3,2,0,1:T(8,128)(2,1)S(1)} %reshape.37), kind=kOutput, calls=%fused_computation.4 | convolution fusion | flops 7084800 | bytes 2384640 | tf_op jit(solution)/shard_map/kab,kbn->kan/dot_general | solution.py:30
  4.9 0.8 copy.19
  5.7 2.0 %reshape.38 = bf16[54,2,40,40]{3,2,0,1:T(8,128)(2,1)S(1)} reshape(bf16[1,54,2,1600]{3,1,2,0:T(8,128)(2,1)} %copy.19) | data formatting | bytes 691200 | tf_op jit(solution)/shard_map/reshape | solution.py:37
  7.7 1.5 %fusion.9 = f32[54,40,40]{2,1,0:T(8,128)S(1)} fusion(bf16[54,40,40]{2,1,0:T(8,128)(2,1)} %fusion, bf16[54,2,40,40]{3,2,0,1:T(8,128)(2,1)S(1)} %reshape.38), kind=kOutput, calls=%fused_computation.21 | convolution fusion | flops 6912000 | bytes 1071360 | tf_op jit(solution)/shard_map/kam,kan->kmn/dot_general | solution.py:30
  10.2 0.8 copy-done.7
  11.0 0.5 fusion.5
  13.1 0.6 copy-done.6
  13.6 0.5 fusion.4
  15.0 1.2 %copy.33 = bf16[16,2,54,2,50]{4,3,2,1,0:T(2,128)(2,1)S(1)} copy(bf16[16,2,54,2,50]{2,4,1,0,3:T(8,128)(2,1)S(1)} %maximum_bitcast_fusion) | data formatting | bytes 691200 | tf_op jit(solution)/shard_map/reshape | solution.py:296
  16.1 0.5 reshape.44
  16.6 0.9 pad.4.refs_0_
  17.5 33.8 %to_pairs.1 = bf16[32,56,128]{2,1,0:T(8,128)(2,1)} custom-call(bf16[32,56,128]{2,1,0:T(8,128)(2,1)} %pad.4.refs_0_), custom_call_target="tpu_custom_call" | custom-call | tf_op jit(solution)/shard_map/to_pairs/pallas_call | solution.py:235
  51.3 1.2 %reshape.40 = bf16[12,144,100]{2,1,0:T(8,128)(2,1)S(1)} reshape(bf16[32,54,100]{2,1,0:T(8,128)(2,1)} %bitcast.51) | data formatting | bytes 691200 | tf_op jit(solution)/shard_map/reshape | solution.py:299
  53.4 0.7 copy.28.phonon_ref
  54.1 3.0 %tables.1 = (s32[32,128]{1,0:T(8,128)}, f32[32,128]{1,0:T(8,128)}, bf16[512,256]{1,0:T(8,128)(2,1)}) custom-call(s32[1,2048]{1,0:T(1,128)} %bitcast.53, s32[3,2048]{1,0:T(4,128)} %bitcast.52, s32[1,2048]{1,0:T(1,128)} %bitcast.54, s32[32,3]{1,0:T(8,128)} %copy.28.phonon_ref), custom_call_target="tpu_custom_call" | custom-call | flops 100000000 | bytes 1000000 | tf_op jit(solution)/shard_map/tables/pallas_call | solution.py:281
  57.1 0.7 copy-done.5
  57.8 6.5 %k_transform.1.refs_0_ = bf16[32,104,128]{2,1,0:T(8,128)(2,1)S(1)} custom-call(bf16[12,288,100]{2,1,0:T(8,128)(2,1)S(1)} %maximum_maximum_fusion.x_ref, bf16[288,288]{1,0:T(8,128)(2,1)S(1)} %copy-done.3, s32[32,128]{1,0:T(8,128)S(1)} %copy-done.5), custom_call_target="tpu_custom_call" | custom-call | tf_op jit(solution)/shard_map/k_transform/pallas_call | solution.py:302
  64.3 0.9 copy-done.1
  65.2 31.1 %to_readers.1.refs_0_ = bf16[32,104,128]{2,1,0:T(8,128)(2,1)} custom-call(bf16[32,104,128]{2,1,0:T(8,128)(2,1)} %copy-done.1), custom_call_target="tpu_custom_call" | custom-call | tf_op jit(solution)/shard_map/to_readers/pallas_call | solution.py:235
  96.3 1.1 %copy-done = bf16[32,104,128]{2,1,0:T(8,128)(2,1)S(1)} copy-done((bf16[32,104,128]{2,1,0:T(8,128)(2,1)S(1)}, bf16[32,104,128]{2,1,0:T(8,128)(2,1)}, u32[]{:S(2)}) %copy-start) | copy-done | bytes 851992
  97.5 3.7 %q_transform.1 = f32[32,200,128]{2,1,0:T(8,128)} custom-call(bf16[32,104,128]{2,1,0:T(8,128)(2,1)S(1)} %copy-done, bf16[512,256]{1,0:T(8,128)(2,1)S(1)} %copy-done.2, f32[32,128]{1,0:T(8,128)S(1)} %copy-done.4), custom_call_target="tpu_custom_call" | custom-call | tf_op jit(solution)/shard_map/q_transform/pallas_call | solution.py:317
  (31 shorter events, 4.6 us)
Async XLA Ops:
  0.0 2.1 %copy-start.9 = (bf16[54,2,1600]{2,1,0:T(2,128)(2,1)S(1)}, bf16[54,2,1600]{2,1,0:T(2,128)(2,1)}, u32[]{:S(2)}) copy-start(bf16[54,2,1600]{2,1,0:T(2,128)(2,1)} %param.9) | copy-start | bytes 1036804
  3.7 1.3 %copy-start.10 = (bf16[1,54,2,1600]{3,2,1,0:T(2,128)(2,1)S(1)}, bf16[1,54,2,1600]{3,2,1,0:T(2,128)(2,1)}, u32[]{:S(2)}) copy-start(bf16[1,54,2,1600]{3,2,1,0:T(2,128)(2,1)} %param.10) | copy-start | bytes 1036804
  10.2 0.8 copy-start.7
  11.5 1.1 %copy-start.8 = (bf16[54,40,40]{2,1,0:T(8,128)(2,1)S(1)}, bf16[54,40,40]{2,1,0:T(8,128)(2,1)}, u32[]{:S(2)}) copy-start(bf16[54,40,40]{2,1,0:T(8,128)(2,1)} %copy-done.7) | copy-start | bytes 518404
  12.6 1.1 %copy-start.6 = (bf16[54,40,40]{2,1,0:T(8,128)(2,1)S(1)}, bf16[54,40,40]{2,1,0:T(8,128)(2,1)}, u32[]{:S(2)}) copy-start(bf16[54,40,40]{2,1,0:T(8,128)(2,1)} %fusion) | copy-start | bytes 518404
  52.7 0.7 copy-start.11
  52.7 4.4 %copy-start.3 = (bf16[288,288]{1,0:T(8,128)(2,1)S(1)}, bf16[288,288]{1,0:T(8,128)(2,1)}, u32[]{:S(2)}) copy-start(bf16[288,288]{1,0:T(8,128)(2,1)} %constant.5.clone.plane_ref) | copy-start | bytes 497668
  57.1 0.7 copy-start.5
  64.3 0.9 copy-start.1
  65.2 31.1 %copy-start.2 = (bf16[512,256]{1,0:T(8,128)(2,1)S(1)}, bf16[512,256]{1,0:T(8,128)(2,1)}, u32[]{:S(2)}) copy-start(bf16[512,256]{1,0:T(8,128)(2,1)} %get-tuple-element.9.refs_1_) | copy-start | bytes 786436
  65.2 31.1 %copy-start.4 = (f32[32,128]{1,0:T(8,128)S(1)}, f32[32,128]{1,0:T(8,128)}, u32[]{:S(2)}) copy-start(f32[32,128]{1,0:T(8,128)} %get-tuple-element.10.refs_2_) | copy-start | bytes 49156
  96.3 1.2 %copy-start = (bf16[32,104,128]{2,1,0:T(8,128)(2,1)S(1)}, bf16[32,104,128]{2,1,0:T(8,128)(2,1)}, u32[]{:S(2)}) copy-start(bf16[32,104,128]{2,1,0:T(8,128)(2,1)} %to_readers.1.refs_0_) | copy-start | bytes 2555908

commit v4 on v3

--- a/solution.py
+++ b/solution.py
@@ -46,7 +46,7 @@
     return jnp.stack([y_real, y_imag], 1).reshape(k_local, 2, W * W).astype(jnp.bfloat16)
 
 
-def table_kernel(reader_ref, vector_ref, degen_ref, phonon_ref, residue_ref, inverse_ref, kron_ref):
+def table_kernel(reader_ref, vector_ref, degen_ref, residue_ref, inverse_ref):
     total_r = reader_ref.shape[1]
     f32, bf16 = jnp.float32, jnp.bfloat16
     reader_id = lax.broadcasted_iota(jnp.int32, (READERS, 128), 0)
@@ -79,6 +79,9 @@
     residue_ref[...] = jnp.where(used, residue, -1.0).astype(jnp.int32)
     inverse_ref[...] = jnp.where(used, 1.0 / jnp.where(used, degen, 1.0), 0.0)
 
+
+def phonon_kernel(phonon_ref, kron_ref):
+    f32, bf16 = jnp.float32, jnp.bfloat16
     rows, columns = kron_ref.shape
     row = lax.broadcasted_iota(jnp.int32, (rows, columns), 0)
     column = lax.broadcasted_iota(jnp.int32, (rows, columns), 1)
@@ -140,7 +143,7 @@
         right = residue_ref[pl.ds(2 * step + 1, 1), :]
         wanted = jnp.concatenate([left, right], axis=1)
         chosen = (row_id == wanted).astype(f32).astype(bf16)
-        found = jnp.dot(t_ref[...], chosen, preferred_element_type=f32)[:104].astype(bf16)
+        found = jnp.dot(t_ref[...], chosen, preferred_element_type=f32)[:width].astype(bf16)
         out_ref[pl.ds(2 * step, 1)] = found[None, :, :128]
         out_ref[pl.ds(2 * step + 1, 1)] = found[None, :, 128:]
         return carry
@@ -148,15 +151,11 @@
     lax.fori_loop(0, READERS // 2, pick, 0)
 
 
-def exchange_kernel(rotated, x_ref, out_ref, send_sem, recv_sem, self_sem):
+def exchange_kernel(x_ref, out_ref, send_sem, recv_sem, self_sem):
     pb, ka = lax.axis_index("pb"), lax.axis_index("ka")
-    source = lax.rem(ka // 2 + 16 - pb, 16) if rotated else pb
+    source = lax.rem(ka // 2 + 16 - pb, 16)
 
     def target(step):
-        if not rotated:
-            shift = lax.rem(13 * step, 32)
-            to = lax.rem(ka // 8 + shift // 8, 4) * 8 + lax.rem(ka + shift, 8)
-            return to, pb, to
         to = lax.rem(pb + 5 * (step // 2), 16)
         half = step % 2
         return 2 * to + half, to, lax.rem(2 * (pb + to) + half, 32)
@@ -186,7 +185,7 @@
         return carry
 
     lax.fori_loop(0, 32, greet, 0)
-    pl.semaphore_wait(barrier, 31 if not rotated else jnp.where(source == pb, 31, 32))
+    pl.semaphore_wait(barrier, jnp.where(source == pb, 31, 32))
 
     def send(step, carry):
         row, to_pb, to_ka = target(step)
@@ -231,9 +230,9 @@
     lax.fori_loop(0, 32, sent, 0)
 
 
-def exchange(x, rotated, number, name):
+def exchange(x, number, name):
     return pl.pallas_call(
-        lambda *refs: exchange_kernel(rotated, *refs),
+        exchange_kernel,
         out_shape=jax.ShapeDtypeStruct(x.shape, x.dtype),
         in_specs=[VMEM],
         out_specs=VMEM,
@@ -278,30 +277,37 @@
     k_local = coupling.shape[1]
     total_r = r_elec.shape[0]
     shape = jax.ShapeDtypeStruct
-    residue, inverse, kron = pl.pallas_call(
+    residue, inverse = pl.pallas_call(
         table_kernel,
         out_shape=(
             shape((READERS, MOST), jnp.int32),
             shape((READERS, MOST), f32),
-            shape((512, 256), bf16),
         ),
-        in_specs=[VMEM] * 4,
-        out_specs=(VMEM,) * 3,
+        in_specs=[VMEM] * 3,
+        out_specs=(VMEM,) * 2,
         cost_estimate=pl.CostEstimate(flops=10**8, bytes_accessed=10**6, transcendentals=0),
         name="tables",
-    )(reader.reshape(1, total_r), r_elec.T, degen.reshape(1, total_r), r_phon)
+    )(reader.reshape(1, total_r), r_elec.T, degen.reshape(1, total_r))
+    kron = pl.pallas_call(
+        phonon_kernel,
+        out_shape=shape((512, 256), bf16),
+        in_specs=[VMEM],
+        out_specs=VMEM,
+        cost_estimate=pl.CostEstimate(flops=10**8, bytes_accessed=10**6, transcendentals=0),
+        name="phonon_table",
+    )(r_phon)
 
     rotated = rotate(coupling, rot_k, rot_kq)
     pieces = rotated.reshape(k_local, 2, 16, 2, 50).transpose(2, 3, 0, 1, 4)
     pieces = pieces.reshape(32, k_local, 100)
     pieces = jnp.pad(pieces, ((0, 0), (0, 56 - k_local), (0, 28)))
-    pieces = exchange(pieces, True, 1, "to_pairs")[:, :k_local, :100]
+    pieces = exchange(pieces, 1, "to_pairs")[:, :k_local, :100]
     x = pieces.reshape(KGRID, PLANE, 100)
     turned = jnp.concatenate([x[:, :, 50:], -x[:, :, :50]], axis=2)
     x = jnp.concatenate([x, turned], axis=1)
     slots = pl.pallas_call(
         k_kernel,
-        out_shape=shape((READERS, 104, MOST), bf16),
+        out_shape=shape((READERS, 100, MOST), bf16),
         in_specs=[VMEM] * 3,
         out_specs=VMEM,
         scratch_shapes=[
@@ -312,14 +318,14 @@
         compiler_params=pltpu.CompilerParams(vmem_limit_bytes=40 * 2**20),
         name="k_transform",
     )(x, jnp.asarray(plane_table()), residue)
-    w = exchange(slots, False, 2, "to_readers")
+    w = lax.all_to_all(slots, "ka", 0, 0, tiled=True)
     groups = 3
     out = pl.pallas_call(
         lambda *refs: q_kernel(groups, *refs),
         grid=(5,),
         out_shape=shape((32, 200, MOST), f32),
         in_specs=[
-            pl.BlockSpec((32, 104, MOST), lambda i: (0, 0, 0)),
+            pl.BlockSpec((32, 100, MOST), lambda i: (0, 0, 0)),
             pl.BlockSpec((512, 256), lambda i: (0, 0)),
             pl.BlockSpec((READERS, MOST), lambda i: (0, 0)),
         ],

time: 102 us -> 103 us (level)
  the two profiles are of different devices: /device:TPU:1 before, /device:TPU:8 now
where the time goes in v4:
time: 103 us; the launch traced here: 102 us
  Pallas kernels  45 us (44%)
  waiting for transfers between devices  21.7 us (21%)
  local copies, waits for them, and re-layouts  16 us (16%)
  starting transfers between devices  11.6 us (11%)
  matrix products  6.89 us (7%)
    pallas_call x1, Pallas kernels, exchange(): pl.pallas_call(exchange_kernel, out_shape=jax.ShapeDtypeStruct(x.shape, x...  29.1 us
    all_to_all x1, waiting for transfers between devices, per_device(): w = lax.all_to_all(slots, 'ka', 0, 0, tiled=True)  21.7 us
    all_to_all x1, starting transfers between devices, per_device(): w = lax.all_to_all(slots, 'ka', 0, 0, tiled=True)  11.6 us
    pallas_call x1, Pallas kernels, per_device(): pl.pallas_call(k_kernel, out_shape=shape((READERS, 100, MOST), bf16), in_...  7.4 us
    dot_general x8, matrix products, product(): return jnp.einsum(spec, left, right, preferred_element_type=jnp.float32)  6.89 us
    unnamed x24, local copies, waits for them, and re-layouts  4.68 us
    pallas_call x1, Pallas kernels, per_device(): pl.pallas_call(lambda *refs: q_kernel(groups, *refs), grid=(5,), out_shap...  3.68 us
    pallas_call x1, Pallas kernels, per_device(): pl.pallas_call(table_kernel, out_shape=(shape((READERS, MOST), jnp.int32)...  2.64 us
  transfers between devices with their start and end apart: 1, of which 1 were waited for; matrix products, arithmetic and copies ran while one was open for 1% of the time, Pallas kernels for 2%

profile of v4, /device:TPU:8, one launch (start us, length us, event | category | flops | bytes accessed | tf_op | source)
XLA Modules:
  0.0 102.2 jit_solution(2051622193201992502)
XLA Ops:
  0.0 1.1 %copy.17 = bf16[1,54,2,1600]{3,1,2,0:T(8,128)(2,1)S(1)} copy(bf16[1,54,2,1600]{3,2,1,0:T(2,128)(2,1)} %param.8) | data formatting | bytes 691200 | tf_op args[0]
  1.1 1.0 %reshape.36 = bf16[54,2,40,40]{3,2,0,1:T(8,128)(2,1)S(1)} reshape(bf16[1,54,2,1600]{3,1,2,0:T(8,128)(2,1)S(1)} %copy.17) | data formatting | bytes 691200 | tf_op jit(solution)/shard_map/reshape | solution.py:35
  2.2 1.0 %reshape.37 = bf16[54,2,40,40]{3,2,0,1:T(8,128)(2,1)S(1)} reshape(bf16[54,2,1600]{2,0,1:T(8,128)(2,1)S(1)} %copy.18) | data formatting | bytes 691200 | tf_op jit(solution)/shard_map/reshape | solution.py:36
  3.7 1.4 %fusion.6 = f32[54,40,40]{2,1,0:T(8,128)} fusion(bf16[54,2,40,40]{3,2,0,1:T(8,128)(2,1)S(1)} %reshape.36, bf16[54,2,40,40]{3,2,0,1:T(8,128)(2,1)S(1)} %reshape.37), kind=kOutput, calls=%fused_computation.18 | convolution fusion | flops 6912000 | bytes 1451520 | tf_op jit(solution)/shard_map/kab,kbn->kan/dot_general | solution.py:30
  5.1 1.3 %fusion = bf16[54,40,40]{2,1,0:T(8,128)(2,1)} fusion(f32[54,40,40]{2,1,0:T(8,128)S(1)} %fusion.7, bf16[54,2,40,40]{3,2,0,1:T(8,128)(2,1)S(1)} %reshape.36, bf16[54,2,40,40]{3,2,0,1:T(8,128)(2,1)S(1)} %reshape.37), kind=kOutput, calls=%fused_computation.4 | convolution fusion | flops 7084800 | bytes 2384640 | tf_op jit(solution)/shard_map/kab,kbn->kan/dot_general | solution.py:30
  6.4 0.8 copy.19
  7.1 2.0 %reshape.38 = bf16[54,2,40,40]{3,2,0,1:T(8,128)(2,1)S(1)} reshape(bf16[1,54,2,1600]{3,1,2,0:T(8,128)(2,1)} %copy.19) | data formatting | bytes 691200 | tf_op jit(solution)/shard_map/reshape | solution.py:37
  9.2 1.7 %fusion.1 = bf16[54,40,40]{2,1,0:T(8,128)(2,1)S(1)} fusion(f32[54,40,40]{2,1,0:T(8,128)} %fusion.6, bf16[54,2,40,40]{3,2,0,1:T(8,128)(2,1)S(1)} %reshape.37, bf16[54,2,40,40]{3,2,0,1:T(8,128)(2,1)S(1)} %reshape.36), kind=kOutput, calls=%fused_computation.5 | convolution fusion | flops 7084800 | bytes 1624320 | tf_op jit(solution)/shard_map/kab,kbn->kan/dot_general | solution.py:30
  11.9 0.5 fusion.5
  12.5 1.2 %copy.22 = bf16[54,40,40]{0,2,1:T(8,128)(2,1)} copy(bf16[54,40,40]{1,2,0:T(8,128)(2,1)S(1)} %fusion.5) | data formatting | bytes 345600 | tf_op jit(solution)/shard_map/add | solution.py:44
  13.7 1.9 %stack.9 = bf16[54,1,16,2,50]{0,4,3,2,1:T(8,128)(2,1)} reshape(bf16[54,40,40]{0,2,1:T(8,128)(2,1)} %copy.22) | data formatting | bytes 345600 | tf_op jit(solution)/shard_map/stack | solution.py:46
  17.4 1.0 copy.33
  18.8 0.9 pad.4.x_ref
  19.7 29.1 %to_pairs.1 = bf16[32,56,128]{2,1,0:T(8,128)(2,1)} custom-call(bf16[32,56,128]{2,1,0:T(8,128)(2,1)} %pad.4.x_ref), custom_call_target="tpu_custom_call" | custom-call | tf_op jit(solution)/shard_map/to_pairs/pallas_call | solution.py:234
  48.9 1.2 %reshape.40 = bf16[12,144,100]{2,1,0:T(8,128)(2,1)S(1)} reshape(bf16[32,54,100]{2,1,0:T(8,128)(2,1)} %bitcast.51) | data formatting | bytes 691200 | tf_op jit(solution)/shard_map/reshape | solution.py:305
  50.6 2.6 %tables.1 = (s32[32,128]{1,0:T(8,128)}, f32[32,128]{1,0:T(8,128)}) custom-call(s32[1,2048]{1,0:T(1,128)} %bitcast.53, s32[3,2048]{1,0:T(4,128)} %bitcast.52, s32[1,2048]{1,0:T(1,128)} %bitcast.54), custom_call_target="tpu_custom_call" | custom-call | flops 100000000 | bytes 1000000 | tf_op jit(solution)/shard_map/tables/pallas_call | solution.py:280
  53.2 0.7 copy-done.3
  53.9 7.4 %k_transform.1 = bf16[32,100,128]{2,1,0:T(8,128)(2,1)} custom-call(bf16[12,288,100]{2,1,0:T(8,128)(2,1)S(1)} %maximum_maximum_fusion.x_ref, bf16[288,288]{1,0:T(8,128)(2,1)S(1)} %copy-done.1, s32[32,128]{1,0:T(8,128)S(1)} %copy-done.3), custom_call_target="tpu_custom_call" | custom-call | tf_op jit(solution)/shard_map/k_transform/pallas_call | solution.py:308
  61.4 11.6 %all-to-all-start = ((bf16[32,100,128]{2,1,0:T(8,128)(2,1)}), bf16[32,100,128]{2,1,0:T(8,128)(2,1)S(1)}, u32[]{:S(2)}, u32[]{:S(2)}) async-start(bf16[32,100,128]{2,1,0:T(8,128)(2,1)} %k_transform.1), calls=%async_computation | async-start | bytes 1703936 | tf_op jit(solution)/shard_map/all_to_all | solution.py:321
  73.0 0.7 copy.28.phonon_ref
  73.7 2.2 %phonon_table.1.refs_1_ = bf16[512,256]{1,0:T(8,128)(2,1)} custom-call(s32[32,3]{1,0:T(8,128)} %copy.28.phonon_ref), custom_call_target="tpu_custom_call" | custom-call | flops 100000000 | bytes 1000000 | tf_op jit(solution)/shard_map/phonon_table/pallas_call | solution.py:291
  75.8 21.7 %all-to-all-done.refs_0_ = bf16[32,100,128]{2,1,0:T(8,128)(2,1)S(1)} async-done(((bf16[32,100,128]{2,1,0:T(8,128)(2,1)}), bf16[32,100,128]{2,1,0:T(8,128)(2,1)S(1)}, u32[]{:S(2)}, u32[]{:S(2)}) %all-to-all-start) | async-done | bytes 819232 | tf_op jit(solution)/shard_map/all_to_all | solution.py:321
  97.5 0.9 copy-done
  98.5 3.7 %q_transform.1 = f32[32,200,128]{2,1,0:T(8,128)} custom-call(bf16[32,100,128]{2,1,0:T(8,128)(2,1)S(1)} %all-to-all-done.refs_0_, bf16[512,256]{1,0:T(8,128)(2,1)S(1)} %copy-done, f32[32,128]{1,0:T(8,128)S(1)} %copy-done.2), custom_call_target="tpu_custom_call" | custom-call | tf_op jit(solution)/shard_map/q_transform/pallas_call | solution.py:323
  (29 shorter events, 4.2 us)
Async XLA Ops:
  0.0 2.1 %copy-start.7 = (bf16[54,2,1600]{2,1,0:T(2,128)(2,1)S(1)}, bf16[54,2,1600]{2,1,0:T(2,128)(2,1)}, u32[]{:S(2)}) copy-start(bf16[54,2,1600]{2,1,0:T(2,128)(2,1)} %param.9) | copy-start | bytes 1036804
  5.1 1.3 %copy-start.8 = (bf16[1,54,2,1600]{3,2,1,0:T(2,128)(2,1)S(1)}, bf16[1,54,2,1600]{3,2,1,0:T(2,128)(2,1)}, u32[]{:S(2)}) copy-start(bf16[1,54,2,1600]{3,2,1,0:T(2,128)(2,1)} %param.10) | copy-start | bytes 1036804
  9.2 1.8 %copy-start.4 = (bf16[54,40,40]{2,1,0:T(8,128)(2,1)S(1)}, bf16[54,40,40]{2,1,0:T(8,128)(2,1)}, u32[]{:S(2)}) copy-start(bf16[54,40,40]{2,1,0:T(8,128)(2,1)} %fusion) | copy-start | bytes 518404
  12.5 3.1 %copy-start.5 = (bf16[54,40,40]{2,1,0:T(8,128)(2,1)S(1)}, bf16[54,40,40]{2,1,0:T(8,128)(2,1)}, u32[]{:S(2)}) copy-start(bf16[54,40,40]{2,1,0:T(8,128)(2,1)} %fusion) | copy-start | bytes 518404
  16.1 1.0 copy-start.6
  50.2 3.0 %copy-start.1 = (bf16[288,288]{1,0:T(8,128)(2,1)S(1)}, bf16[288,288]{1,0:T(8,128)(2,1)}, u32[]{:S(2)}) copy-start(bf16[288,288]{1,0:T(8,128)(2,1)} %constant.5.clone.plane_ref) | copy-start | bytes 497668
  53.2 0.7 copy-start.3
  61.4 11.6 %copy-start.9 = (s32[32,3]{0,1:T(4,128)S(1)}, s32[32,3]{0,1:T(4,128)}, u32[]{:S(2)}) copy-start(s32[32,3]{0,1:T(4,128)} %param.14) | copy-start | bytes 1156
  61.4 36.2 %copy-start.2 = (f32[32,128]{1,0:T(8,128)S(1)}, f32[32,128]{1,0:T(8,128)}, u32[]{:S(2)}) copy-start(f32[32,128]{1,0:T(8,128)} %get-tuple-element.8.refs_2_) | copy-start | bytes 49156
  61.4 36.2 %all-to-all-start = ((bf16[32,100,128]{2,1,0:T(8,128)(2,1)}), bf16[32,100,128]{2,1,0:T(8,128)(2,1)S(1)}, u32[]{:S(2)}, u32[]{:S(2)}) async-start(bf16[32,100,128]{2,1,0:T(8,128)(2,1)} %k_transform.1), calls=%async_computation | async-start | bytes 1703936 | tf_op jit(solution)/shard_map/all_to_all | solution.py:321
  97.5 1.0 copy-start
